TPU v7x, 256 devices: a whole 4x4x8 slice. The times are simulated.
256 devices in a mesh: leaf: 32 (over y, z), panel: 8 (over x, core).
Axes of the slice: x: 4, y: 4, z: 8, core: 2. Of those that a mesh axis runs over, the one named last changes fastest.
Arguments:
- child_front: float32 [32, 2, 8, 128, 2048], P('leaf', None, 'panel'), as said below
- parent_entries: float32 [32, 4, 8, 128, 512], P('leaf', None, 'panel'), as said below
- parent_of: int32 [32], replicated, may hold values from 0 to 31
- owner_slot: int32 [32], replicated, may hold values from 0 to 31, each once
- front_blocks: int32 [32], replicated, may hold values from 8 to 32, as said below
- block_lists: int32 [32, 8], replicated, may hold values from 0 to 31, as said below
Outputs:
- child_factor: float32 [32, 2, 8, 128, 1024], P('leaf', None, 'panel')
- parent_factor: float32 [32, 4, 8, 128, 512], P('leaf', None, 'panel')
Inputs may be any that keep to these rules, and one draw needn't show every extreme that they name: `front_blocks`: each entry is a multiple of the panel axis size; the largest equals 32. `block_lists`: the entries of a row are distinct, each below front_blocks of the child's parent, and entry k leaves the same remainder as k when divided by the panel axis size. `child_front`: symmetric, with a positive definite leading block of every front. `parent_entries`: the leading 512 rows form a symmetric positive definite block.
All inputs are finite; a program needn't handle non-finite values.
Results may differ from a plain program's by a relative error of at most 0.00044.
Values may be sent and summed in bfloat16 or wider, within the bound.
No kernel may reach another device: no remote copies, remote signals or barrier semaphores. Data moves between devices by JAX's collectives and lax.ppermute only.
A program may use at most 128 MiB of HBM per device.

v0:
```python
import functools

import jax
import jax.numpy as jnp
from jax import lax
from jax.experimental import pallas as pl
from jax.experimental.pallas import tpu as pltpu
from jax.sharding import PartitionSpec as P

BLK = 128
PANEL = 512
WC = 2048
PC = 1024
CBB = 8
NB = PANEL // BLK
SUB = 8
TILE = 16
TILES = BLK // TILE * NB
F32 = jnp.float32
BF16 = jnp.bfloat16


def split(a):
    hi = a.astype(BF16)
    return hi, (a - hi.astype(F32)).astype(BF16)


def dot_nn(a, b):
    return lax.dot_general(a, b, (((1,), (0,)), ((), ())), preferred_element_type=F32)


def dot_nt(a, b):
    return lax.dot_general(a, b, (((1,), (1,)), ((), ())), preferred_element_type=F32)


def mm(dot, a, b):
    (ah, al), (bh, bl) = a, b
    return dot(ah, bh) + (dot(al, bh) + dot(ah, bl))


def lanes(v, j):
    return jnp.broadcast_to(v[:, j : j + 1], (SUB, BLK))


def sublanes(v, k):
    return jnp.broadcast_to(v[k : k + 1, :], (SUB, BLK))


def total(terms):
    while len(terms) > 1:
        terms = [a + b for a, b in zip(terms[::2], terms[1::2])] + terms[len(terms) // 2 * 2 :]
    return terms[0]


def factor_block(block, one):
    count = BLK // SUB
    span = count // 2
    width = span * SUB
    sub = lax.broadcasted_iota(jnp.int32, (SUB, BLK), 0)
    lane = lax.broadcasted_iota(jnp.int32, (SUB, BLK), 1)
    rows = [block[SUB * i : SUB * (i + 1), :] for i in range(count)]
    out = [None] * count
    for half in range(2):
        base = half * span
        now = rows[base : base + span]
        cols = None
        for g in range(span):
            first = SUB * (base + g)
            inside = (lane >= first) & (lane < first + SUB)
            follows = g + 1 < span
            if cols is None:
                cols = [lanes(now[g], first + k) * one for k in range(SUB)]
            if follows:
                kept = [lanes(now[g + 1], first + k) for k in range(SUB)]
                after = [lanes(now[g + 1], first + SUB + k) for k in range(SUB)]
                weights = [w * one for w in kept]
            head = jnp.where(inside, jnp.where(lane == first + sub, 1.0, 0.0), now[g])
            done = jnp.zeros((SUB, BLK), F32)
            for k in range(SUB):
                across = [sublanes(cols[q], k) if q >= k else None for q in range(SUB)]
                inv = 1.0 / across[k]
                here = sub == k
                row = sublanes(head, k)
                for q in range(k + 1, SUB):
                    step = jnp.where(here, -across[q], cols[k] * across[q])
                    cols[q] = jnp.where(here, 0.0, cols[q]) - step * inv
                step = jnp.where(here, -row, cols[k] * row)
                done = jnp.where(here, row * lax.rsqrt(across[k]), done)
                head = jnp.where(here, 0.0, head) - step * inv
                if follows:
                    scaled = weights[k] * inv
                    for q in range(k + 1, SUB):
                        weights[q] = weights[q] - scaled * across[q]
                    for q in range(SUB):
                        after[q] = after[q] - scaled * sublanes(weights[k], q)
            out[base + g] = done
            if base + g == count - 1:
                break
            spread = [sublanes(head, k) for k in range(SUB)]
            others = list(range(g + 1, span)) + (list(range(g)) if half == 0 else [])
            for i in others:
                mult = kept if i == g + 1 else [lanes(now[i], first + k) for k in range(SUB)]
                now[i] = jnp.where(inside, 0.0, now[i]) - total([m * r for m, r in zip(mult, spread)])
            now[g] = head
            cols = after if follows else None
        if half == 0:
            below = jnp.concatenate(rows[span:], axis=0)
            solved = jnp.concatenate(now + [jnp.zeros((BLK - width, BLK), F32)], axis=0)
            left = lax.broadcasted_iota(jnp.int32, below.shape, 1) < width
            below = jnp.where(left, 0.0, below) - mm(dot_nn, split(below), split(solved))
            rows[span:] = [below[SUB * i : SUB * (i + 1), :] for i in range(count - span)]
    return jnp.concatenate(out, axis=0)


def invert_panel(at, work, beside=None):
    row = lax.broadcasted_iota(jnp.int32, (BLK, BLK), 0)
    col = lax.broadcasted_iota(jnp.int32, (BLK, BLK), 1)
    lane_block = lax.broadcasted_iota(jnp.int32, (BLK, PANEL), 1) // BLK
    one = jnp.full((SUB, BLK), 1.0, F32) * jnp.minimum(at[2], 1).astype(F32)

    def step(b, carry):
        here = pl.ds(pl.multiple_of(b * BLK, BLK), BLK)
        if beside is not None:
            beside(b)
        inv = jnp.where(row >= col, factor_block(work[b, :, here], one), 0.0)
        inv = split(inv) + (inv,)
        across = mm(dot_nn, inv[:2], split(work[b]))
        across = jnp.where(lane_block == b, jnp.concatenate([inv[2]] * NB, axis=1), across)
        across_parts = split(across)
        work[b] = across
        for i in range(1, NB):

            @pl.when(i > b)
            def _():
                below = split(mm(dot_nt, split(work[i, :, here]), inv[:2]))
                kept = jnp.where(lane_block == b, 0.0, work[i])
                work[i] = kept - mm(dot_nn, below, across_parts)

        return carry

    lax.fori_loop(0, NB, step, 0)


def lower_parts(work, parts, flipped=None):
    lane_block = lax.broadcasted_iota(jnp.int32, (BLK, PANEL), 1) // BLK
    for i in range(NB):
        rows = slice(i * BLK, (i + 1) * BLK)
        lower = jnp.where(lane_block <= i, work[i], 0.0)
        parts[0, rows, :], parts[1, rows, :] = split(lower)
        if flipped is not None:
            for j in range(NB):
                flip = split(lower[:, j * BLK : (j + 1) * BLK].T)
                for p in range(2):
                    flipped[p, j * BLK : (j + 1) * BLK, rows] = flip[p]


def take_pivot(at, blocks, work, sem=None):
    core = at[1] % 2

    for chip, own in enumerate(((0, 1), (1, 0), (3, 2), (2, 3))):

        @pl.when(at[1] // 2 == chip)
        def _():
            for i in range(2):
                for k in range(2):
                    source, to = blocks[4 * k + own[i]], work.at[2 * i + (core + k) % 2]
                    if sem is None:
                        to[...] = source[...]
                    else:
                        pltpu.make_async_copy(source, to, sem).start()

    if sem is not None:
        pltpu.make_async_copy(work, work, sem).wait()


def first_kernel(at, b0, b1, b2, b3, b4, b5, b6, b7, inv_out, work, inv, sem):
    take_pivot(at, (b0, b1, b2, b3, b4, b5, b6, b7), work, sem)
    invert_panel(at, work)
    lower_parts(work, inv.at[0], inv.at[1])
    copy = pltpu.make_async_copy(inv, inv_out, sem)
    copy.start()
    copy.wait()


def pair(ref, rows=slice(None)):
    return ref[0, rows, :], ref[1, rows, :]


def child_kernel(at, mid, own, inv0, factor, contribution, work, inv1, above, low_first, low_second, rows_second, own_first):
    upper = mid[NB:, :, :PANEL].reshape(PANEL, PANEL)
    upper_parts = split(upper)
    solved = split(mm(dot_nt, upper_parts, pair(inv0.at[0])))
    flipped = split(mm(dot_nt, pair(inv0.at[0]), upper_parts))
    above[0], above[1] = flipped
    second = mid[NB:, :, PANEL:].reshape(PANEL, PANEL) - mm(dot_nn, solved, flipped)
    work[...] = second.reshape(NB, BLK, PANEL)
    chunk = 2 * BLK // NB

    def beside(b):
        to = pl.ds(pl.multiple_of(b * BLK, BLK), BLK)
        part = split(mm(dot_nn, split(mid[b, :, :PANEL]), pair(inv0.at[1])))
        low_first[0, to, :], low_first[1, to, :] = part
        rows_second[to, :] = mid[b, :, PANEL:] - mm(dot_nn, part, pair(above))
        s = b // 2
        rows = pl.ds(pl.multiple_of((b % 2) * chunk, chunk), chunk)
        first = mm(dot_nn, split(own[s, rows, :PANEL]), pair(inv0.at[1]))
        factor[s, rows, :PANEL] = first
        part = split(first)
        to = pl.ds(pl.multiple_of(b * chunk, chunk), chunk)
        own_first[0, to, :], own_first[1, to, :] = part
        to = pl.ds(pl.multiple_of(PANEL + b * chunk, chunk), chunk)
        rows_second[to, :] = own[s, rows, PANEL:PC] - mm(dot_nn, part, pair(above))

    invert_panel(at, work, beside)
    lower_parts(work, inv1)
    result = mm(dot_nt, split(rows_second[...]), pair(inv1))
    low_second[0], low_second[1] = split(result[:PANEL])
    second = result[PANEL + BLK :]
    rest = own[1, :, PC : PC + PANEL] - mm(dot_nt, pair(own_first, slice(BLK, None)), pair(low_first))
    rest = (rest - mm(dot_nt, split(second), pair(low_second))).astype(BF16)
    for i in range(TILES):
        r, k = i // NB * TILE, i % NB * BLK
        contribution[i] = rest[r : r + TILE, k : k + BLK]
    factor[0, :, PANEL:] = jnp.where(at[1] < NB, 0.0, result[PANEL : PANEL + BLK])
    factor[1, :, PANEL:] = second


def pack_kernel(at, parent_of, owner_slot, tiles, out, count):
    def clear(s, carry):
        count[s] = 0
        return carry

    def place(c, carry):
        slot = owner_slot[parent_of[c]]
        out[slot, count[slot]] = tiles[c]
        count[slot] = count[slot] + 1
        return carry

    lax.fori_loop(0, out.shape[0], clear, 0)
    lax.fori_loop(0, tiles.shape[0], place, 0)


def assemble_kernel(at, parent_of, owner_slot, front_blocks, block_lists, entries, tiles, out, pivot):
    leaf = at[0]

    def find(q, live):
        return jnp.where(owner_slot[q] == leaf, front_blocks[q], live)

    live = lax.fori_loop(0, owner_slot.shape[0], find, jnp.int32(0))
    for t in range(entries.shape[0]):
        alive = t * at[2] + at[1] < live
        out[t] = jnp.where(alive, entries[t], 0.0)

    def add(c, k):
        hit = owner_slot[parent_of[c]] == leaf

        @pl.when(hit)
        def _():
            t = block_lists[c, at[1]] // at[2]
            for b in range(NB):

                @pl.when(block_lists[c, b] == b)
                def _():
                    for i in range(b, TILES, NB):
                        rows, cols = slice(i // NB * TILE, (i // NB + 1) * TILE), slice(b * BLK, (b + 1) * BLK)
                        out[t, rows, cols] = out[t, rows, cols] + tiles[i, k].astype(F32)

        return k + hit.astype(jnp.int32)

    lax.fori_loop(0, parent_of.shape[0], add, jnp.int32(0))
    pivot[...] = out[0]


def parent_kernel(at, b0, b1, b2, b3, b4, b5, b6, b7, rows, factor, work, inv):
    take_pivot(at, (b0, b1, b2, b3, b4, b5, b6, b7), work)
    invert_panel(at, work)
    lower_parts(work, inv)
    slots = rows.shape[0]
    solved = mm(dot_nt, split(rows[...].reshape(slots * BLK, PANEL)), pair(inv))
    factor[...] = solved.reshape(slots, BLK, PANEL)


VMEM = pl.BlockSpec(memory_space=pltpu.VMEM)
SMEM = pl.BlockSpec(memory_space=pltpu.SMEM)
ANY = pl.BlockSpec(memory_space=pl.ANY)
HBM = pl.BlockSpec(memory_space=pltpu.HBM)


def limit(mib):
    return pltpu.CompilerParams(vmem_limit_bytes=mib * 1024 * 1024)


def shape(*dims, dtype=F32):
    return jax.ShapeDtypeStruct(dims, dtype)


def chip_permute(x, pairs):
    return lax.ppermute(x, "panel", [(2 * a + c, 2 * b + c) for a, b in pairs for c in range(2)])


def gather_pivot(block):
    near = chip_permute(block, ((0, 1), (1, 0)))
    next_ = chip_permute(block, ((0, 3), (1, 2)))
    far = chip_permute(block, ((0, 2), (1, 3)))
    blocks = (block, near, next_, far)
    return blocks + tuple(lax.ppermute(b, "panel", [(i, i ^ 1) for i in range(8)]) for b in blocks)


def add_children(depth, at, tables, entries, tiles):
    parent_of, owner_slot, front_blocks, block_lists = tables
    sends = pl.pallas_call(
        pack_kernel,
        out_shape=shape(TILES, depth, TILE, BLK, dtype=BF16),
        in_specs=[SMEM, SMEM, SMEM, VMEM],
        out_specs=VMEM,
        scratch_shapes=[pltpu.SMEM((TILES,), jnp.int32)],
        compiler_params=limit(8),
        name=f"pack{depth}",
    )(at, parent_of, owner_slot, tiles)
    mine = lax.all_to_all(sends, "leaf", 0, 0, tiled=True)
    return pl.pallas_call(
        assemble_kernel,
        out_shape=(shape(*entries.shape), shape(BLK, PANEL)),
        in_specs=[SMEM, SMEM, SMEM, SMEM, SMEM, VMEM, VMEM],
        out_specs=(VMEM, VMEM),
        compiler_params=limit(12),
        name=f"assemble{depth}",
    )(at, parent_of, owner_slot, front_blocks, block_lists, entries, mine)


def on_device(child_front, parent_entries, parent_of, owner_slot, front_blocks, block_lists):
    panel_count = lax.axis_size("panel")
    panel = lax.axis_index("panel")
    leaf = lax.axis_index("leaf")
    parent_slots = parent_entries.shape[1]
    own = child_front.reshape(2, BLK, WC)
    with jax.named_scope("mid"):
        slot = (panel < NB).astype(jnp.int32)
        one = lax.dynamic_slice(own, (slot, jnp.int32(0), jnp.int32(0)), (1, BLK, PC))
        mid = lax.all_gather(one, "panel", axis=0, tiled=True)
    with jax.named_scope("pivot0"):
        blocks = gather_pivot(own[0, :, :PANEL])
    at = jnp.stack([leaf, panel, panel_count]).astype(jnp.int32)
    work = pltpu.VMEM((NB, BLK, PANEL), F32)
    parts = pltpu.VMEM((2, PANEL, PANEL), BF16)
    inv0 = pl.pallas_call(
        first_kernel,
        out_shape=shape(2, 2, PANEL, PANEL, dtype=BF16),
        in_specs=[SMEM] + [ANY] * 8,
        out_specs=HBM,
        scratch_shapes=[work, pltpu.VMEM((2, 2, PANEL, PANEL), BF16), pltpu.SemaphoreType.DMA],
        compiler_params=limit(12),
        name="first_panel",
    )(at, *[pltpu.with_memory_space_constraint(b, pltpu.HBM) for b in blocks])
    factor, contribution = pl.pallas_call(
        child_kernel,
        out_shape=(shape(2, BLK, PC), shape(TILES, TILE, BLK, dtype=BF16)),
        in_specs=[SMEM, VMEM, VMEM, VMEM],
        out_specs=(VMEM, VMEM),
        scratch_shapes=[
            work,
            parts,
            parts,
            parts,
            parts,
            pltpu.VMEM((PANEL + 2 * BLK, PANEL), F32),
            pltpu.VMEM((2, 2 * BLK, PANEL), BF16),
        ],
        compiler_params=limit(28),
        name="child",
    )(at, mid, own, inv0)
    slots = jnp.sum(jnp.where(parent_of[:, None] == jnp.arange(owner_slot.shape[0])[None, :], owner_slot[None, :], 0), axis=1)
    most = jnp.max(jnp.sum((slots[:, None] == jnp.arange(TILES)[None, :]).astype(jnp.int32), axis=0))
    with jax.named_scope("tiles"):
        tiles = lax.all_to_all(contribution, "leaf", 0, 0, tiled=True)
    tables = (parent_of, owner_slot, front_blocks, block_lists)
    depths = (4, 6, parent_of.shape[0])
    with jax.named_scope("children"):
        assembled, pivot = lax.switch(
            (most > depths[0]).astype(jnp.int32) + (most > depths[1]).astype(jnp.int32),
            [lambda e, r, d=d: add_children(d, at, tables, e, r) for d in depths],
            parent_entries.reshape(parent_slots, BLK, PANEL),
            tiles,
        )
    with jax.named_scope("pivot2"):
        blocks = gather_pivot(pivot)
    parent_factor = pl.pallas_call(
        parent_kernel,
        out_shape=shape(parent_slots, BLK, PANEL),
        in_specs=[SMEM] + [VMEM] * 9,
        out_specs=VMEM,
        scratch_shapes=[
            work,
            parts,
        ],
        compiler_params=limit(14),
        name="parent",
    )(at, *blocks, assembled)
    return (factor.reshape(child_front.shape[:-1] + (PC,)), parent_factor.reshape(parent_entries.shape))


def solution(mesh):
    front = P("leaf", None, "panel", None, None)
    return jax.shard_map(
        on_device,
        mesh=mesh,
        in_specs=(front, front, P(), P(), P(), P()),
        out_specs=(front, front),
        check_vma=False,
    )
```

profile of v0, /device:TPU:39, one launch (start us, length us, event | category | flops | bytes accessed | tf_op | source)
XLA Modules:
  0.0 164.7 jit_solution(10749610569803562766)
XLA Ops:
  7.2 1.9 %constant_dynamic-slice_fusion = f32[1,1,1,128,1024]{4,3,2,1,0:T(8,128)} fusion(f32[1,2,1,128,2048]{4,3,2,1,0:T(8,128)} %param.9, s32[]{:T(128)S(6)} %select_n.7), kind=kLoop, calls=%fused_computation.6 | loop fusion | bytes 1048580 | tf_op jit(solution)/shard_map/mid/dynamic_slice | solution.py:339
  9.1 1.0 slice_bitcast_fusion.b0
  10.8 1.3 collective-permute-start.1
  12.1 1.3 collective-permute-start.2
  14.3 12.4 %collective-permute-done.1.b2 = f32[128,512]{1,0:T(8,128)S(1)} collective-permute-done((f32[128,512]{1,0:T(8,128)S(1)}, f32[128,512]{1,0:T(8,128)S(1)}, u32[]{:S(2)}, u32[]{:S(2)}) %collective-permute-start.1) | collective-permute-done | bytes 262176 | tf_op jit(solution)/shard_map/pivot0/ppermute | solution.py:298
  26.7 2.0 %collective-permute-start.5 = (f32[128,512]{1,0:T(8,128)S(1)}, f32[128,512]{1,0:T(8,128)S(1)}, u32[]{:S(2)}, u32[]{:S(2)}) collective-permute-start(f32[128,512]{1,0:T(8,128)S(1)} %collective-permute-done.1.b2), channel_id=1, source_target_pairs={{0,1},{1,0},{2,3},{3,2},{4,5},{5,4},{6,7},{7,6},{8,9},{9,8},{10,11... | collective-permute-start | bytes 786440 | tf_op jit(solution)/shard_map/pivot0/ppermute | solution.py:306
  30.6 15.6 %first_panel.1.inv0 = bf16[2,2,512,512]{3,2,1,0:T(8,128)(2,1)S(1)} custom-call(s32[3]{0:T(128)S(1)} %pad_add_fusion.at, f32[128,512]{1,0:T(8,128)} %copy-done.4, f32[128,512]{1,0:T(8,128)} %copy-done.5, f32[128,512]{1,0:T(8,128)} %copy-done.6, f32[128,512]{1,0:T(8,128)} %copy-done.7, f32[128,512]{1,0:T(8,128)} %copy-done.8, f32[128,512]{1,0:T(8,128)} %copy-done.9, ...), custom_call_target="tpu_custom_call" | custom-call | tf_op jit(solution)/shard_map/first_panel/pallas_call | solution.py:346
  46.4 2.2 %copy-done.1 = f32[8,1,1,128,1024]{4,3,2,1,0:T(8,128)S(1)} copy-done((f32[8,1,1,128,1024]{4,3,2,1,0:T(8,128)S(1)}, f32[8,1,1,128,1024]{4,3,2,1,0:T(8,128)}, u32[]{:S(2)}) %copy-start.1) | copy-done | bytes 4194328
  48.6 1.6 copy-done.2
  50.2 20.6 %child.1 = (f32[2,128,1024]{2,1,0:T(8,128)}, bf16[32,16,128]{2,1,0:T(8,128)(2,1)}) custom-call(s32[3]{0:T(128)S(1)} %pad_add_fusion.at, f32[8,128,1024]{2,1,0:T(8,128)S(1)} %bitcast.13, f32[2,128,2048]{2,1,0:T(8,128)S(1)} %bitcast.15, bf16[2,2,512,512]{3,2,1,0:T(8,128)(2,1)S(1)} %first_panel.1.inv0), custom_call_target="tpu_custom_call" | custom-call | tf_op jit(solution)/shard_map/child/pallas_call | solution.py:355
  70.9 12.8 %all-to-all-start.3 = ((bf16[32,16,128]{2,1,0:T(8,128)(2,1)}), bf16[32,16,128]{2,1,0:T(8,128)(2,1)S(1)}, u32[]{:S(2)}, u32[]{:S(2)}) async-start(bf16[32,16,128]{2,1,0:T(8,128)(2,1)} %get-tuple-element.70), calls=%async_computation.3 | async-start | bytes 262144 | tf_op jit(solution)/shard_map/tiles/all_to_all | solution.py:375
  86.0 6.4 %all-to-all-done.3 = bf16[32,16,128]{2,1,0:T(8,128)(2,1)S(1)} async-done(((bf16[32,16,128]{2,1,0:T(8,128)(2,1)}), bf16[32,16,128]{2,1,0:T(8,128)(2,1)S(1)}, u32[]{:S(2)}, u32[]{:S(2)}) %all-to-all-start.3) | async-done | bytes 131104 | tf_op jit(solution)/shard_map/tiles/all_to_all | solution.py:375
  92.5 29.5 %conditional.1 = ((f32[4,128,512]{2,1,0:T(8,128)S(1)}, f32[128,512]{1,0:T(8,128)S(1)})) conditional(s32[]{:T(128)} %clamp.3, (s32[3]{0:T(128)S(1)}, s32[32]{0:T(128)S(1)}, s32[32]{0:T(128)S(1)}, bf16[32,16,128]{2,1,0:T(8,128)(2,1)S(1)}, s32[32]{0:T(128)S(1)}, /*index=5*/s32[32,8]{0,1:T(8,128)S(1)}, ...), branch_computations={%region_3.4_spmd, %region_4.5_spmd, %region_5.6_spmd} | conditional | bytes 29362244 | solution.py:379
  92.5 2.0 %pack6.1 = bf16[32,6,16,128]{3,2,1,0:T(8,128)(2,1)} custom-call(s32[3]{0:T(128)S(1)} %get-tuple-element.49.at, s32[32]{0:T(128)S(1)} %get-tuple-element.50.parent_of, s32[32]{0:T(128)S(1)} %get-tuple-element.51.owner_slot, bf16[32,16,128]{2,1,0:T(8,128)(2,1)S(1)} %get-tuple-element.55.tiles), custom_call_target="tpu_custom_call" | custom-call | tf_op jit(solution)/shard_map/children/cond/branch_1_fun/pack6/pallas_call | solution.py:311
  94.5 4.7 %all-to-all-start.1 = ((bf16[32,6,16,128]{3,2,1,0:T(8,128)(2,1)}), bf16[32,6,16,128]{3,2,1,0:T(8,128)(2,1)S(1)}, u32[]{:S(2)}, u32[]{:S(2)}) async-start(bf16[32,6,16,128]{3,2,1,0:T(8,128)(2,1)} %pack6.1), calls=%async_computation.1 | async-start | bytes 1572864 | tf_op jit(solution)/shard_map/children/cond/branch_1_fun/all_to_all | solution.py:320
  99.3 20.6 %all-to-all-done.1.tiles = bf16[32,6,16,128]{3,2,1,0:T(8,128)(2,1)S(1)} async-done(((bf16[32,6,16,128]{3,2,1,0:T(8,128)(2,1)}), bf16[32,6,16,128]{3,2,1,0:T(8,128)(2,1)S(1)}, u32[]{:S(2)}, u32[]{:S(2)}) %all-to-all-start.1) | async-done | bytes 786464 | tf_op jit(solution)/shard_map/children/cond/branch_1_fun/all_to_all | solution.py:320
  119.9 1.9 %assemble6.1 = (f32[4,128,512]{2,1,0:T(8,128)S(1)}, f32[128,512]{1,0:T(8,128)S(1)}) custom-call(s32[3]{0:T(128)S(1)} %get-tuple-element.49.at, s32[32]{0:T(128)S(1)} %get-tuple-element.50.parent_of, s32[32]{0:T(128)S(1)} %get-tuple-element.51.owner_slot, s32[32]{0:T(128)S(1)} %get-tuple-element.52.front_blocks, s32[32,8]{1,0:T(8,128)S(1)} %copy.20.block_lists, ...), custom_call_target="tpu_custom_call" | custom-call | tf_op jit(solution)/shard_map/children/cond/branch_1_fun/assemble6/pallas_call | solution.py:321
  122.7 1.3 collective-permute-start.8
  124.0 1.3 collective-permute-start.9
  125.3 3.8 %collective-permute-start.10 = (f32[128,512]{1,0:T(8,128)S(1)}, f32[128,512]{1,0:T(8,128)S(1)}, u32[]{:S(2)}, u32[]{:S(2)}) collective-permute-start(f32[128,512]{1,0:T(8,128)S(1)} %get-tuple-element.71.b0), channel_id=1, source_target_pairs={{0,1},{1,0},{2,3},{3,2},{4,5},{5,4},{6,7},{7,6},{8,9},{9,8},{10,11... | collective-permute-start | bytes 786440 | tf_op jit(solution)/shard_map/pivot2/ppermute | solution.py:306
  129.2 3.0 %collective-permute-done.8.b2 = f32[128,512]{1,0:T(8,128)S(1)} collective-permute-done((f32[128,512]{1,0:T(8,128)S(1)}, f32[128,512]{1,0:T(8,128)S(1)}, u32[]{:S(2)}, u32[]{:S(2)}) %collective-permute-start.8) | collective-permute-done | bytes 262176 | tf_op jit(solution)/shard_map/pivot2/ppermute | solution.py:298
  132.2 8.0 %collective-permute-start.12 = (f32[128,512]{1,0:T(8,128)S(1)}, f32[128,512]{1,0:T(8,128)S(1)}, u32[]{:S(2)}, u32[]{:S(2)}) collective-permute-start(f32[128,512]{1,0:T(8,128)S(1)} %collective-permute-done.8.b2), channel_id=1, source_target_pairs={{0,1},{1,0},{2,3},{3,2},{4,5},{5,4},{6,7},{7,6},{8,9},{9,8},{10,11... | collective-permute-start | bytes 786440 | tf_op jit(solution)/shard_map/pivot2/ppermute | solution.py:306
  140.2 1.1 collective-permute-done.12.b6
  141.8 16.1 %parent.1 = f32[4,128,512]{2,1,0:T(8,128)} custom-call(s32[3]{0:T(128)S(1)} %pad_add_fusion.at, f32[128,512]{1,0:T(8,128)S(1)} %get-tuple-element.71.b0, f32[128,512]{1,0:T(8,128)S(1)} %collective-permute-done.7.b1, f32[128,512]{1,0:T(8,128)S(1)} %collective-permute-done.8.b2, f32[128,512]{1,0:T(8,128)S(1)} %collective-permute-done.9.b3, ...), custom_call_target="tpu_custom_call" | custom-call | tf_op jit(solution)/shard_map/parent/pallas_call | solution.py:387
  (52 shorter events, 5.9 us)
Async XLA Ops:
  7.2 39.2 %all-gather.3.cloned.1.call-start = ((), (), s32[]{:S(2)}) async-start(), calls=%async_computation.4 | async-start | bytes 4718592 | tf_op jit(solution)/shard_map/mid/all_gather | solution.py:340
  10.1 20.4 %copy-start.4 = (f32[128,512]{1,0:T(8,128)}, f32[128,512]{1,0:T(8,128)S(1)}, u32[]{:S(2)}) copy-start(f32[128,512]{1,0:T(8,128)S(1)} %slice_bitcast_fusion.b0) | copy-start | bytes 786436
  10.1 4.1 %collective-permute-start = (f32[128,512]{1,0:T(8,128)S(1)}, f32[128,512]{1,0:T(8,128)S(1)}, u32[]{:S(2)}, u32[]{:S(2)}) collective-permute-start(f32[128,512]{1,0:T(8,128)S(1)} %slice_bitcast_fusion.b0), channel_id=1, source_target_pairs={{0,2},{1,3},{2,0},{3,1},{8,10},{9,11},{10,8},{11,9},{16,18},{17,19... | collective-permute-start | bytes 786440 | tf_op jit(solution)/shard_map/pivot0/ppermute | solution.py:298
  10.8 15.9 %collective-permute-start.1 = (f32[128,512]{1,0:T(8,128)S(1)}, f32[128,512]{1,0:T(8,128)S(1)}, u32[]{:S(2)}, u32[]{:S(2)}) collective-permute-start(f32[128,512]{1,0:T(8,128)S(1)} %slice_bitcast_fusion.b0), channel_id=1, source_target_pairs={{0,6},{1,7},{2,4},{3,5},{8,14},{9,15},{10,12},{11,13},{16,22},{17,... | collective-permute-start | bytes 786440 | tf_op jit(solution)/shard_map/pivot0/ppermute | solution.py:298
  12.1 16.6 %collective-permute-start.2 = (f32[128,512]{1,0:T(8,128)S(1)}, f32[128,512]{1,0:T(8,128)S(1)}, u32[]{:S(2)}, u32[]{:S(2)}) collective-permute-start(f32[128,512]{1,0:T(8,128)S(1)} %slice_bitcast_fusion.b0), channel_id=1, source_target_pairs={{0,4},{1,5},{2,6},{3,7},{8,12},{9,13},{10,14},{11,15},{16,20},{17,... | collective-permute-start | bytes 786440 | tf_op jit(solution)/shard_map/pivot0/ppermute | solution.py:298
  13.4 15.6 %collective-permute-start.3 = (f32[128,512]{1,0:T(8,128)S(1)}, f32[128,512]{1,0:T(8,128)S(1)}, u32[]{:S(2)}, u32[]{:S(2)}) collective-permute-start(f32[128,512]{1,0:T(8,128)S(1)} %slice_bitcast_fusion.b0), channel_id=1, source_target_pairs={{0,1},{1,0},{2,3},{3,2},{4,5},{5,4},{6,7},{7,6},{8,9},{9,8},{10,11... | collective-permute-start | bytes 786440 | tf_op jit(solution)/shard_map/pivot0/ppermute | solution.py:306
  14.2 16.4 %copy-start.5 = (f32[128,512]{1,0:T(8,128)}, f32[128,512]{1,0:T(8,128)S(1)}, u32[]{:S(2)}) copy-start(f32[128,512]{1,0:T(8,128)S(1)} %collective-permute-done.b1) | copy-start | bytes 786436
  14.2 14.9 %collective-permute-start.4 = (f32[128,512]{1,0:T(8,128)S(1)}, f32[128,512]{1,0:T(8,128)S(1)}, u32[]{:S(2)}, u32[]{:S(2)}) collective-permute-start(f32[128,512]{1,0:T(8,128)S(1)} %collective-permute-done.b1), channel_id=1, source_target_pairs={{0,1},{1,0},{2,3},{3,2},{4,5},{5,4},{6,7},{7,6},{8,9},{9,8},{10,11... | collective-permute-start | bytes 786440 | tf_op jit(solution)/shard_map/pivot0/ppermute | solution.py:306
  26.7 3.1 %collective-permute-start.5 = (f32[128,512]{1,0:T(8,128)S(1)}, f32[128,512]{1,0:T(8,128)S(1)}, u32[]{:S(2)}, u32[]{:S(2)}) collective-permute-start(f32[128,512]{1,0:T(8,128)S(1)} %collective-permute-done.1.b2), channel_id=1, source_target_pairs={{0,1},{1,0},{2,3},{3,2},{4,5},{5,4},{6,7},{7,6},{8,9},{9,8},{10,11... | collective-permute-start | bytes 786440 | tf_op jit(solution)/shard_map/pivot0/ppermute | solution.py:306
  28.7 1.9 %collective-permute-start.6 = (f32[128,512]{1,0:T(8,128)S(1)}, f32[128,512]{1,0:T(8,128)}, u32[]{:S(2)}, u32[]{:S(2)}) collective-permute-start(f32[128,512]{1,0:T(8,128)S(1)} %collective-permute-done.2.b3), channel_id=1, source_target_pairs={{0,1},{1,0},{2,3},{3,2},{4,5},{5,4},{6,7},{7,6},{8,9},{9,8},{10,11... | collective-permute-start | bytes 786440 | tf_op jit(solution)/shard_map/pivot0/ppermute | solution.py:306
  50.2 33.5 %copy-start.12 = (s32[32]{0:T(128)S(1)}, s32[32]{0:T(128)}, u32[]{:S(2)}) copy-start(s32[32]{0:T(128)} %param.12) | copy-start | bytes 388
  50.2 33.5 %copy-start.13 = (s32[32]{0:T(128)S(1)}, s32[32]{0:T(128)}, u32[]{:S(2)}) copy-start(s32[32]{0:T(128)} %param.11) | copy-start | bytes 388
  50.2 42.3 %copy-start.3 = (f32[1,4,1,128,512]{4,3,2,1,0:T(8,128)S(1)}, f32[1,4,1,128,512]{4,3,2,1,0:T(8,128)}, u32[]{:S(2)}) copy-start(f32[1,4,1,128,512]{4,3,2,1,0:T(8,128)} %param.10) | copy-start | bytes 3145732
  50.2 42.3 %copy-start.11 = (s32[32,8]{0,1:T(8,128)S(1)}, s32[32,8]{0,1:T(8,128)}, u32[]{:S(2)}) copy-start(s32[32,8]{0,1:T(8,128)} %param.14) | copy-start | bytes 3076
  50.2 42.3 %copy-start.14 = (s32[32]{0:T(128)S(1)}, s32[32]{0:T(128)}, u32[]{:S(2)}) copy-start(s32[32]{0:T(128)} %param.13) | copy-start | bytes 388
  70.9 21.6 %all-to-all-start.3 = ((bf16[32,16,128]{2,1,0:T(8,128)(2,1)}), bf16[32,16,128]{2,1,0:T(8,128)(2,1)S(1)}, u32[]{:S(2)}, u32[]{:S(2)}) async-start(bf16[32,16,128]{2,1,0:T(8,128)(2,1)} %get-tuple-element.70), calls=%async_computation.3 | async-start | bytes 262144 | tf_op jit(solution)/shard_map/tiles/all_to_all | solution.py:375
  94.5 25.4 %all-to-all-start.1 = ((bf16[32,6,16,128]{3,2,1,0:T(8,128)(2,1)}), bf16[32,6,16,128]{3,2,1,0:T(8,128)(2,1)S(1)}, u32[]{:S(2)}, u32[]{:S(2)}) async-start(bf16[32,6,16,128]{3,2,1,0:T(8,128)(2,1)} %pack6.1), calls=%async_computation.1 | async-start | bytes 1572864 | tf_op jit(solution)/shard_map/children/cond/branch_1_fun/all_to_all | solution.py:320
  122.0 7.1 %collective-permute-start.7 = (f32[128,512]{1,0:T(8,128)S(1)}, f32[128,512]{1,0:T(8,128)S(1)}, u32[]{:S(2)}, u32[]{:S(2)}) collective-permute-start(f32[128,512]{1,0:T(8,128)S(1)} %get-tuple-element.71.b0), channel_id=1, source_target_pairs={{0,2},{1,3},{2,0},{3,1},{8,10},{9,11},{10,8},{11,9},{16,18},{17,19... | collective-permute-start | bytes 786440 | tf_op jit(solution)/shard_map/pivot2/ppermute | solution.py:298
  122.7 9.5 %collective-permute-start.8 = (f32[128,512]{1,0:T(8,128)S(1)}, f32[128,512]{1,0:T(8,128)S(1)}, u32[]{:S(2)}, u32[]{:S(2)}) collective-permute-start(f32[128,512]{1,0:T(8,128)S(1)} %get-tuple-element.71.b0), channel_id=1, source_target_pairs={{0,6},{1,7},{2,4},{3,5},{8,14},{9,15},{10,12},{11,13},{16,22},{17,... | collective-permute-start | bytes 786440 | tf_op jit(solution)/shard_map/pivot2/ppermute | solution.py:298
  124.0 16.2 %collective-permute-start.9 = (f32[128,512]{1,0:T(8,128)S(1)}, f32[128,512]{1,0:T(8,128)S(1)}, u32[]{:S(2)}, u32[]{:S(2)}) collective-permute-start(f32[128,512]{1,0:T(8,128)S(1)} %get-tuple-element.71.b0), channel_id=1, source_target_pairs={{0,4},{1,5},{2,6},{3,7},{8,12},{9,13},{10,14},{11,15},{16,20},{17,... | collective-permute-start | bytes 786440 | tf_op jit(solution)/shard_map/pivot2/ppermute | solution.py:298
  125.3 14.9 %collective-permute-start.10 = (f32[128,512]{1,0:T(8,128)S(1)}, f32[128,512]{1,0:T(8,128)S(1)}, u32[]{:S(2)}, u32[]{:S(2)}) collective-permute-start(f32[128,512]{1,0:T(8,128)S(1)} %get-tuple-element.71.b0), channel_id=1, source_target_pairs={{0,1},{1,0},{2,3},{3,2},{4,5},{5,4},{6,7},{7,6},{8,9},{9,8},{10,11... | collective-permute-start | bytes 786440 | tf_op jit(solution)/shard_map/pivot2/ppermute | solution.py:306
  129.1 11.1 %collective-permute-start.11 = (f32[128,512]{1,0:T(8,128)S(1)}, f32[128,512]{1,0:T(8,128)S(1)}, u32[]{:S(2)}, u32[]{:S(2)}) collective-permute-start(f32[128,512]{1,0:T(8,128)S(1)} %collective-permute-done.7.b1), channel_id=1, source_target_pairs={{0,1},{1,0},{2,3},{3,2},{4,5},{5,4},{6,7},{7,6},{8,9},{9,8},{10,11... | collective-permute-start | bytes 786440 | tf_op jit(solution)/shard_map/pivot2/ppermute | solution.py:306
  132.2 9.1 %collective-permute-start.12 = (f32[128,512]{1,0:T(8,128)S(1)}, f32[128,512]{1,0:T(8,128)S(1)}, u32[]{:S(2)}, u32[]{:S(2)}) collective-permute-start(f32[128,512]{1,0:T(8,128)S(1)} %collective-permute-done.8.b2), channel_id=1, source_target_pairs={{0,1},{1,0},{2,3},{3,2},{4,5},{5,4},{6,7},{7,6},{8,9},{9,8},{10,11... | collective-permute-start | bytes 786440 | tf_op jit(solution)/shard_map/pivot2/ppermute | solution.py:306
  140.2 1.5 collective-permute-start.13
  (7 other events, 12.5 us)
Sparse Core Ops, SparseCore 0:
  10.4 35.9 all-gather.2
where the time goes:
time: 163 us; the launch traced here: 165 us
  Pallas kernels  56.3 us (35%)
  waiting for transfers between devices  45 us (28%)
  starting transfers between devices  39.1 us (24%)
  between operations  15.6 us (10%)
  local copies, waits for them, and re-layouts  7.45 us (5%)
    pallas_call x1, Pallas kernels, on_device(): pl.pallas_call(child_kernel, out_shape=(shape(2, BLK, PC), shape(TILES, T...  20.6 us
    all_to_all x1, waiting for transfers between devices, add_children(): mine = lax.all_to_all(sends, 'leaf', 0, 0, tiled=True)  20.6 us
    pallas_call x1, Pallas kernels, on_device(): pl.pallas_call(parent_kernel, out_shape=shape(parent_slots, BLK, PANEL),...  16.1 us
    pallas_call x1, Pallas kernels, on_device(): pl.pallas_call(first_kernel, out_shape=shape(2, 2, PANEL, PANEL, dtype=BF...  15.6 us
    ppermute x6, waiting for transfers between devices, chip_permute(): lax.ppermute(x, 'panel', [(2 * a + c, 2 * b + c) for a, b in pairs for c...  15.4 us
    ppermute x8, starting transfers between devices, gather_pivot(): lax.ppermute(b, 'panel', [(i, i ^ 1) for i in range(8)])  15 us
    all_to_all x1, starting transfers between devices, on_device(): tiles = lax.all_to_all(contribution, 'leaf', 0, 0, tiled=True)  12.8 us
    ppermute x6, starting transfers between devices, chip_permute(): lax.ppermute(x, 'panel', [(2 * a + c, 2 * b + c) for a, b in pairs for c...  6.52 us
  transfers between devices with their start and end apart: 17, of which 8 were waited for; matrix products, arithmetic and copies ran while one was open for 1% of the time, Pallas kernels for 9%

commit v1 on v0

--- a/solution.py
+++ b/solution.py
@@ -116,6 +116,8 @@
     row = lax.broadcasted_iota(jnp.int32, (BLK, BLK), 0)
     col = lax.broadcasted_iota(jnp.int32, (BLK, BLK), 1)
     lane_block = lax.broadcasted_iota(jnp.int32, (BLK, PANEL), 1) // BLK
+    row_block = lax.broadcasted_iota(jnp.int32, (PANEL - BLK, 1), 0) // BLK + 1
+    later_block = lax.broadcasted_iota(jnp.int32, (PANEL - BLK, PANEL), 1) // BLK
     one = jnp.full((SUB, BLK), 1.0, F32) * jnp.minimum(at[2], 1).astype(F32)
 
     def step(b, carry):
@@ -128,13 +130,14 @@
         across = jnp.where(lane_block == b, jnp.concatenate([inv[2]] * NB, axis=1), across)
         across_parts = split(across)
         work[b] = across
-        for i in range(1, NB):
-
-            @pl.when(i > b)
-            def _():
-                below = split(mm(dot_nt, split(work[i, :, here]), inv[:2]))
-                kept = jnp.where(lane_block == b, 0.0, work[i])
-                work[i] = kept - mm(dot_nn, below, across_parts)
+
+        @pl.when(b < NB - 1)
+        def _():
+            later = work[1:].reshape(PANEL - BLK, PANEL)
+            mine = work[1:, :, here].reshape(PANEL - BLK, BLK)
+            below = jnp.where(row_block > b, mm(dot_nt, split(mine), inv[:2]), 0.0)
+            kept = jnp.where((row_block > b) & (later_block == b), 0.0, later)
+            work[1:] = (kept - mm(dot_nn, split(below), across_parts)).reshape(NB - 1, BLK, PANEL)
 
         return carry
 
@@ -186,7 +189,9 @@
     return ref[0, rows, :], ref[1, rows, :]
 
 
-def child_kernel(at, mid, own, inv0, factor, contribution, work, inv1, above, low_first, low_second, rows_second, own_first):
+def child_kernel(at, mid, own_far, inv0, factor, contribution, own, work, inv1, above, low_first, low_second, rows_second, own_first, sem):
+    fetch = pltpu.make_async_copy(own_far.at[:, :, : PC + PANEL], own, sem)
+    fetch.start()
     upper = mid[NB:, :, :PANEL].reshape(PANEL, PANEL)
     upper_parts = split(upper)
     solved = split(mm(dot_nt, upper_parts, pair(inv0.at[0])))
@@ -195,6 +200,7 @@
     second = mid[NB:, :, PANEL:].reshape(PANEL, PANEL) - mm(dot_nn, solved, flipped)
     work[...] = second.reshape(NB, BLK, PANEL)
     chunk = 2 * BLK // NB
+    fetch.wait()
 
     def beside(b):
         to = pl.ds(pl.multiple_of(b * BLK, BLK), BLK)
@@ -355,9 +361,10 @@
     factor, contribution = pl.pallas_call(
         child_kernel,
         out_shape=(shape(2, BLK, PC), shape(TILES, TILE, BLK, dtype=BF16)),
-        in_specs=[SMEM, VMEM, VMEM, VMEM],
+        in_specs=[SMEM, VMEM, HBM, VMEM],
         out_specs=(VMEM, VMEM),
         scratch_shapes=[
+            pltpu.VMEM((2, BLK, PC + PANEL), F32),
             work,
             parts,
             parts,
@@ -365,10 +372,11 @@
             parts,
             pltpu.VMEM((PANEL + 2 * BLK, PANEL), F32),
             pltpu.VMEM((2, 2 * BLK, PANEL), BF16),
+            pltpu.SemaphoreType.DMA,
         ],
         compiler_params=limit(28),
         name="child",
-    )(at, mid, own, inv0)
+    )(at, mid, pltpu.with_memory_space_constraint(own, pltpu.HBM), inv0)
     slots = jnp.sum(jnp.where(parent_of[:, None] == jnp.arange(owner_slot.shape[0])[None, :], owner_slot[None, :], 0), axis=1)
     most = jnp.max(jnp.sum((slots[:, None] == jnp.arange(TILES)[None, :]).astype(jnp.int32), axis=0))
     with jax.named_scope("tiles"):

time: 163 us -> 159 us (0.975); the launches traced: 165 us -> 156 us
  waiting for transfers between devices: 45 us -> 41.8 us
  Pallas kernels: 56.3 us -> 54 us
  starting transfers between devices: 39.1 us -> 37.2 us
    all_to_all x1, waiting for transfers between devices: 20.6 us -> 15.6 us  [add_children(): mine = lax.all_to_all(sends, 'leaf', 0, 0, tiled=True)]
    unnamed x28 -> x26, local copies, waits for them, and re-layouts: 4.51 us -> 2.94 us
  transfers between devices with their start and end apart: 17 -> 17, of which waited for: 8 -> 8; matrix products, arithmetic and copies ran while one was open for 1% -> 1% of each run, Pallas kernels for 9% -> 10%
where the time goes in v1:
time: 159 us; the launch traced here: 156 us
  Pallas kernels  54 us (34%)
  waiting for transfers between devices  41.8 us (26%)
  starting transfers between devices  37.2 us (23%)
  between operations  15.6 us (10%)
  local copies, waits for them, and re-layouts  5.87 us (4%)
    pallas_call x1, Pallas kernels, on_device(): pl.pallas_call(child_kernel, out_shape=(shape(2, BLK, PC), shape(TILES, T...  20 us
    ppermute x6, waiting for transfers between devices, chip_permute(): lax.ppermute(x, 'panel', [(2 * a + c, 2 * b + c) for a, b in pairs for c...  16.6 us
    all_to_all x1, waiting for transfers between devices, add_children(): mine = lax.all_to_all(sends, 'leaf', 0, 0, tiled=True)  15.6 us
    pallas_call x1, Pallas kernels, on_device(): pl.pallas_call(parent_kernel, out_shape=shape(parent_slots, BLK, PANEL),...  15.4 us
    pallas_call x1, Pallas kernels, on_device(): pl.pallas_call(first_kernel, out_shape=shape(2, 2, PANEL, PANEL, dtype=BF...  14.9 us
    ppermute x8, starting transfers between devices, gather_pivot(): lax.ppermute(b, 'panel', [(i, i ^ 1) for i in range(8)])  13.8 us
    all_to_all x1, starting transfers between devices, on_device(): tiles = lax.all_to_all(contribution, 'leaf', 0, 0, tiled=True)  12.1 us
    ppermute x6, starting transfers between devices, chip_permute(): lax.ppermute(x, 'panel', [(2 * a + c, 2 * b + c) for a, b in pairs for c...  6.52 us
  transfers between devices with their start and end apart: 17, of which 8 were waited for; matrix products, arithmetic and copies ran while one was open for 1% of the time, Pallas kernels for 10%

profile of v1, /device:TPU:39, one launch (start us, length us, event | category | flops | bytes accessed | tf_op | source)
XLA Modules:
  0.0 155.8 jit_solution(10710328580296211501)
XLA Ops:
  7.2 1.9 %constant_dynamic-slice_fusion = f32[1,1,1,128,1024]{4,3,2,1,0:T(8,128)} fusion(f32[1,2,1,128,2048]{4,3,2,1,0:T(8,128)} %param.9, s32[]{:T(128)S(6)} %select_n.7), kind=kLoop, calls=%fused_computation.6 | loop fusion | bytes 1048580 | tf_op jit(solution)/shard_map/mid/dynamic_slice | solution.py:345
  9.1 1.0 slice_bitcast_fusion.b0
  10.8 1.3 collective-permute-start.1
  12.1 1.3 collective-permute-start.2
  14.3 12.4 %collective-permute-done.1.b2 = f32[128,512]{1,0:T(8,128)S(1)} collective-permute-done((f32[128,512]{1,0:T(8,128)S(1)}, f32[128,512]{1,0:T(8,128)S(1)}, u32[]{:S(2)}, u32[]{:S(2)}) %collective-permute-start.1) | collective-permute-done | bytes 262176 | tf_op jit(solution)/shard_map/pivot0/ppermute | solution.py:304
  26.7 2.0 %collective-permute-start.5 = (f32[128,512]{1,0:T(8,128)S(1)}, f32[128,512]{1,0:T(8,128)S(1)}, u32[]{:S(2)}, u32[]{:S(2)}) collective-permute-start(f32[128,512]{1,0:T(8,128)S(1)} %collective-permute-done.1.b2), channel_id=1, source_target_pairs={{0,1},{1,0},{2,3},{3,2},{4,5},{5,4},{6,7},{7,6},{8,9},{9,8},{10,11... | collective-permute-start | bytes 786440 | tf_op jit(solution)/shard_map/pivot0/ppermute | solution.py:312
  30.6 14.9 %first_panel.1.inv0 = bf16[2,2,512,512]{3,2,1,0:T(8,128)(2,1)S(1)} custom-call(s32[3]{0:T(128)S(1)} %pad_add_fusion.at, f32[128,512]{1,0:T(8,128)} %copy-done.3, f32[128,512]{1,0:T(8,128)} %copy-done.4, f32[128,512]{1,0:T(8,128)} %copy-done.5, f32[128,512]{1,0:T(8,128)} %copy-done.6, f32[128,512]{1,0:T(8,128)} %copy-done.7, f32[128,512]{1,0:T(8,128)} %copy-done.8, ...), custom_call_target="tpu_custom_call" | custom-call | tf_op jit(solution)/shard_map/first_panel/pallas_call | solution.py:352
  45.5 0.9 all-gather.3.cloned.1.call-done
  46.4 2.2 %copy-done.1 = f32[8,1,1,128,1024]{4,3,2,1,0:T(8,128)S(1)} copy-done((f32[8,1,1,128,1024]{4,3,2,1,0:T(8,128)S(1)}, f32[8,1,1,128,1024]{4,3,2,1,0:T(8,128)}, u32[]{:S(2)}) %copy-start.1) | copy-done | bytes 4194328
  48.6 20.0 %child.1 = (f32[2,128,1024]{2,1,0:T(8,128)}, bf16[32,16,128]{2,1,0:T(8,128)(2,1)}) custom-call(s32[3]{0:T(128)S(1)} %pad_add_fusion.at, f32[8,128,1024]{2,1,0:T(8,128)S(1)} %bitcast.13, f32[2,128,2048]{2,1,0:T(8,128)} %bitcast.18, bf16[2,2,512,512]{3,2,1,0:T(8,128)(2,1)S(1)} %first_panel.1.inv0), custom_call_target="tpu_custom_call" | custom-call | tf_op jit(solution)/shard_map/child/pallas_call | solution.py:361
  68.6 12.1 %all-to-all-start.3 = ((bf16[32,16,128]{2,1,0:T(8,128)(2,1)}), bf16[32,16,128]{2,1,0:T(8,128)(2,1)S(1)}, u32[]{:S(2)}, u32[]{:S(2)}) async-start(bf16[32,16,128]{2,1,0:T(8,128)(2,1)} %get-tuple-element.70), calls=%async_computation.3 | async-start | bytes 262144 | tf_op jit(solution)/shard_map/tiles/all_to_all | solution.py:383
  83.0 6.4 %all-to-all-done.3 = bf16[32,16,128]{2,1,0:T(8,128)(2,1)S(1)} async-done(((bf16[32,16,128]{2,1,0:T(8,128)(2,1)}), bf16[32,16,128]{2,1,0:T(8,128)(2,1)S(1)}, u32[]{:S(2)}, u32[]{:S(2)}) %all-to-all-start.3) | async-done | bytes 131104 | tf_op jit(solution)/shard_map/tiles/all_to_all | solution.py:383
  89.5 24.3 %conditional.1 = ((f32[4,128,512]{2,1,0:T(8,128)S(1)}, f32[128,512]{1,0:T(8,128)S(1)})) conditional(s32[]{:T(128)} %clamp.3, (s32[3]{0:T(128)S(1)}, s32[32]{0:T(128)S(1)}, s32[32]{0:T(128)S(1)}, bf16[32,16,128]{2,1,0:T(8,128)(2,1)S(1)}, s32[32]{0:T(128)S(1)}, /*index=5*/s32[32,8]{0,1:T(8,128)S(1)}, ...), branch_computations={%region_3.4_spmd, %region_4.5_spmd, %region_5.6_spmd} | conditional | bytes 29362244 | solution.py:387
  89.5 1.9 %pack4.1 = bf16[32,4,16,128]{3,2,1,0:T(8,128)(2,1)} custom-call(s32[3]{0:T(128)S(1)} %get-tuple-element.42.at, s32[32]{0:T(128)S(1)} %get-tuple-element.43.parent_of, s32[32]{0:T(128)S(1)} %get-tuple-element.44.owner_slot, bf16[32,16,128]{2,1,0:T(8,128)(2,1)S(1)} %get-tuple-element.48.tiles), custom_call_target="tpu_custom_call" | custom-call | tf_op jit(solution)/shard_map/children/cond/branch_0_fun/pack4/pallas_call | solution.py:317
  91.4 4.7 %all-to-all-start = ((bf16[32,4,16,128]{3,2,1,0:T(8,128)(2,1)}), bf16[32,4,16,128]{3,2,1,0:T(8,128)(2,1)S(1)}, u32[]{:S(2)}, u32[]{:S(2)}) async-start(bf16[32,4,16,128]{3,2,1,0:T(8,128)(2,1)} %pack4.1), calls=%async_computation | async-start | bytes 1048576 | tf_op jit(solution)/shard_map/children/cond/branch_0_fun/all_to_all | solution.py:326
  96.2 15.6 %all-to-all-done.tiles = bf16[32,4,16,128]{3,2,1,0:T(8,128)(2,1)S(1)} async-done(((bf16[32,4,16,128]{3,2,1,0:T(8,128)(2,1)}), bf16[32,4,16,128]{3,2,1,0:T(8,128)(2,1)S(1)}, u32[]{:S(2)}, u32[]{:S(2)}) %all-to-all-start) | async-done | bytes 524320 | tf_op jit(solution)/shard_map/children/cond/branch_0_fun/all_to_all | solution.py:326
  111.8 1.8 %assemble4.1 = (f32[4,128,512]{2,1,0:T(8,128)S(1)}, f32[128,512]{1,0:T(8,128)S(1)}) custom-call(s32[3]{0:T(128)S(1)} %get-tuple-element.42.at, s32[32]{0:T(128)S(1)} %get-tuple-element.43.parent_of, s32[32]{0:T(128)S(1)} %get-tuple-element.44.owner_slot, s32[32]{0:T(128)S(1)} %get-tuple-element.45.front_blocks, s32[32,8]{1,0:T(8,128)S(1)} %copy.19.block_lists, ...), custom_call_target="tpu_custom_call" | custom-call | tf_op jit(solution)/shard_map/children/cond/branch_0_fun/assemble4/pallas_call | solution.py:327
  114.5 1.3 collective-permute-start.8
  115.8 1.3 collective-permute-start.9
  117.1 3.3 %collective-permute-start.10 = (f32[128,512]{1,0:T(8,128)S(1)}, f32[128,512]{1,0:T(8,128)S(1)}, u32[]{:S(2)}, u32[]{:S(2)}) collective-permute-start(f32[128,512]{1,0:T(8,128)S(1)} %get-tuple-element.71.b0), channel_id=1, source_target_pairs={{0,1},{1,0},{2,3},{3,2},{4,5},{5,4},{6,7},{7,6},{8,9},{9,8},{10,11... | collective-permute-start | bytes 786440 | tf_op jit(solution)/shard_map/pivot2/ppermute | solution.py:312
  120.5 4.2 %collective-permute-done.8.b2 = f32[128,512]{1,0:T(8,128)S(1)} collective-permute-done((f32[128,512]{1,0:T(8,128)S(1)}, f32[128,512]{1,0:T(8,128)S(1)}, u32[]{:S(2)}, u32[]{:S(2)}) %collective-permute-start.8) | collective-permute-done | bytes 262176 | tf_op jit(solution)/shard_map/pivot2/ppermute | solution.py:304
  124.7 7.3 %collective-permute-start.12 = (f32[128,512]{1,0:T(8,128)S(1)}, f32[128,512]{1,0:T(8,128)S(1)}, u32[]{:S(2)}, u32[]{:S(2)}) collective-permute-start(f32[128,512]{1,0:T(8,128)S(1)} %collective-permute-done.8.b2), channel_id=1, source_target_pairs={{0,1},{1,0},{2,3},{3,2},{4,5},{5,4},{6,7},{7,6},{8,9},{9,8},{10,11... | collective-permute-start | bytes 786440 | tf_op jit(solution)/shard_map/pivot2/ppermute | solution.py:312
  132.0 1.1 collective-permute-done.12.b6
  133.5 15.4 %parent.1 = f32[4,128,512]{2,1,0:T(8,128)} custom-call(s32[3]{0:T(128)S(1)} %pad_add_fusion.at, f32[128,512]{1,0:T(8,128)S(1)} %get-tuple-element.71.b0, f32[128,512]{1,0:T(8,128)S(1)} %collective-permute-done.7.b1, f32[128,512]{1,0:T(8,128)S(1)} %collective-permute-done.8.b2, f32[128,512]{1,0:T(8,128)S(1)} %collective-permute-done.9.b3, ...), custom_call_target="tpu_custom_call" | custom-call | tf_op jit(solution)/shard_map/parent/pallas_call | solution.py:395
  (50 shorter events, 5.7 us)
Async XLA Ops:
  7.2 39.2 %all-gather.3.cloned.1.call-start = ((), (), s32[]{:S(2)}) async-start(), calls=%async_computation.4 | async-start | bytes 4718592 | tf_op jit(solution)/shard_map/mid/all_gather | solution.py:346
  10.1 20.4 %copy-start.3 = (f32[128,512]{1,0:T(8,128)}, f32[128,512]{1,0:T(8,128)S(1)}, u32[]{:S(2)}) copy-start(f32[128,512]{1,0:T(8,128)S(1)} %slice_bitcast_fusion.b0) | copy-start | bytes 786436
  10.1 4.1 %collective-permute-start = (f32[128,512]{1,0:T(8,128)S(1)}, f32[128,512]{1,0:T(8,128)S(1)}, u32[]{:S(2)}, u32[]{:S(2)}) collective-permute-start(f32[128,512]{1,0:T(8,128)S(1)} %slice_bitcast_fusion.b0), channel_id=1, source_target_pairs={{0,2},{1,3},{2,0},{3,1},{8,10},{9,11},{10,8},{11,9},{16,18},{17,19... | collective-permute-start | bytes 786440 | tf_op jit(solution)/shard_map/pivot0/ppermute | solution.py:304
  10.8 15.9 %collective-permute-start.1 = (f32[128,512]{1,0:T(8,128)S(1)}, f32[128,512]{1,0:T(8,128)S(1)}, u32[]{:S(2)}, u32[]{:S(2)}) collective-permute-start(f32[128,512]{1,0:T(8,128)S(1)} %slice_bitcast_fusion.b0), channel_id=1, source_target_pairs={{0,6},{1,7},{2,4},{3,5},{8,14},{9,15},{10,12},{11,13},{16,22},{17,... | collective-permute-start | bytes 786440 | tf_op jit(solution)/shard_map/pivot0/ppermute | solution.py:304
  12.1 16.6 %collective-permute-start.2 = (f32[128,512]{1,0:T(8,128)S(1)}, f32[128,512]{1,0:T(8,128)S(1)}, u32[]{:S(2)}, u32[]{:S(2)}) collective-permute-start(f32[128,512]{1,0:T(8,128)S(1)} %slice_bitcast_fusion.b0), channel_id=1, source_target_pairs={{0,4},{1,5},{2,6},{3,7},{8,12},{9,13},{10,14},{11,15},{16,20},{17,... | collective-permute-start | bytes 786440 | tf_op jit(solution)/shard_map/pivot0/ppermute | solution.py:304
  13.4 15.6 %collective-permute-start.3 = (f32[128,512]{1,0:T(8,128)S(1)}, f32[128,512]{1,0:T(8,128)S(1)}, u32[]{:S(2)}, u32[]{:S(2)}) collective-permute-start(f32[128,512]{1,0:T(8,128)S(1)} %slice_bitcast_fusion.b0), channel_id=1, source_target_pairs={{0,1},{1,0},{2,3},{3,2},{4,5},{5,4},{6,7},{7,6},{8,9},{9,8},{10,11... | collective-permute-start | bytes 786440 | tf_op jit(solution)/shard_map/pivot0/ppermute | solution.py:312
  14.2 16.4 %copy-start.4 = (f32[128,512]{1,0:T(8,128)}, f32[128,512]{1,0:T(8,128)S(1)}, u32[]{:S(2)}) copy-start(f32[128,512]{1,0:T(8,128)S(1)} %collective-permute-done.b1) | copy-start | bytes 786436
  14.2 14.9 %collective-permute-start.4 = (f32[128,512]{1,0:T(8,128)S(1)}, f32[128,512]{1,0:T(8,128)S(1)}, u32[]{:S(2)}, u32[]{:S(2)}) collective-permute-start(f32[128,512]{1,0:T(8,128)S(1)} %collective-permute-done.b1), channel_id=1, source_target_pairs={{0,1},{1,0},{2,3},{3,2},{4,5},{5,4},{6,7},{7,6},{8,9},{9,8},{10,11... | collective-permute-start | bytes 786440 | tf_op jit(solution)/shard_map/pivot0/ppermute | solution.py:312
  26.7 3.1 %collective-permute-start.5 = (f32[128,512]{1,0:T(8,128)S(1)}, f32[128,512]{1,0:T(8,128)S(1)}, u32[]{:S(2)}, u32[]{:S(2)}) collective-permute-start(f32[128,512]{1,0:T(8,128)S(1)} %collective-permute-done.1.b2), channel_id=1, source_target_pairs={{0,1},{1,0},{2,3},{3,2},{4,5},{5,4},{6,7},{7,6},{8,9},{9,8},{10,11... | collective-permute-start | bytes 786440 | tf_op jit(solution)/shard_map/pivot0/ppermute | solution.py:312
  28.7 1.9 %collective-permute-start.6 = (f32[128,512]{1,0:T(8,128)S(1)}, f32[128,512]{1,0:T(8,128)}, u32[]{:S(2)}, u32[]{:S(2)}) collective-permute-start(f32[128,512]{1,0:T(8,128)S(1)} %collective-permute-done.2.b3), channel_id=1, source_target_pairs={{0,1},{1,0},{2,3},{3,2},{4,5},{5,4},{6,7},{7,6},{8,9},{9,8},{10,11... | collective-permute-start | bytes 786440 | tf_op jit(solution)/shard_map/pivot0/ppermute | solution.py:312
  48.6 32.1 %copy-start.11 = (s32[32]{0:T(128)S(1)}, s32[32]{0:T(128)}, u32[]{:S(2)}) copy-start(s32[32]{0:T(128)} %param.12) | copy-start | bytes 388
  48.6 32.1 %copy-start.12 = (s32[32]{0:T(128)S(1)}, s32[32]{0:T(128)}, u32[]{:S(2)}) copy-start(s32[32]{0:T(128)} %param.11) | copy-start | bytes 388
  48.6 40.9 %copy-start.2 = (f32[1,4,1,128,512]{4,3,2,1,0:T(8,128)S(1)}, f32[1,4,1,128,512]{4,3,2,1,0:T(8,128)}, u32[]{:S(2)}) copy-start(f32[1,4,1,128,512]{4,3,2,1,0:T(8,128)} %param.10) | copy-start | bytes 3145732
  48.6 40.9 %copy-start.10 = (s32[32,8]{0,1:T(8,128)S(1)}, s32[32,8]{0,1:T(8,128)}, u32[]{:S(2)}) copy-start(s32[32,8]{0,1:T(8,128)} %param.14) | copy-start | bytes 3076
  48.6 40.9 %copy-start.13 = (s32[32]{0:T(128)S(1)}, s32[32]{0:T(128)}, u32[]{:S(2)}) copy-start(s32[32]{0:T(128)} %param.13) | copy-start | bytes 388
  68.6 20.9 %all-to-all-start.3 = ((bf16[32,16,128]{2,1,0:T(8,128)(2,1)}), bf16[32,16,128]{2,1,0:T(8,128)(2,1)S(1)}, u32[]{:S(2)}, u32[]{:S(2)}) async-start(bf16[32,16,128]{2,1,0:T(8,128)(2,1)} %get-tuple-element.70), calls=%async_computation.3 | async-start | bytes 262144 | tf_op jit(solution)/shard_map/tiles/all_to_all | solution.py:383
  91.4 20.4 %all-to-all-start = ((bf16[32,4,16,128]{3,2,1,0:T(8,128)(2,1)}), bf16[32,4,16,128]{3,2,1,0:T(8,128)(2,1)S(1)}, u32[]{:S(2)}, u32[]{:S(2)}) async-start(bf16[32,4,16,128]{3,2,1,0:T(8,128)(2,1)} %pack4.1), calls=%async_computation | async-start | bytes 1048576 | tf_op jit(solution)/shard_map/children/cond/branch_0_fun/all_to_all | solution.py:326
  113.8 6.6 %collective-permute-start.7 = (f32[128,512]{1,0:T(8,128)S(1)}, f32[128,512]{1,0:T(8,128)S(1)}, u32[]{:S(2)}, u32[]{:S(2)}) collective-permute-start(f32[128,512]{1,0:T(8,128)S(1)} %get-tuple-element.71.b0), channel_id=1, source_target_pairs={{0,2},{1,3},{2,0},{3,1},{8,10},{9,11},{10,8},{11,9},{16,18},{17,19... | collective-permute-start | bytes 786440 | tf_op jit(solution)/shard_map/pivot2/ppermute | solution.py:304
  114.5 10.1 %collective-permute-start.8 = (f32[128,512]{1,0:T(8,128)S(1)}, f32[128,512]{1,0:T(8,128)S(1)}, u32[]{:S(2)}, u32[]{:S(2)}) collective-permute-start(f32[128,512]{1,0:T(8,128)S(1)} %get-tuple-element.71.b0), channel_id=1, source_target_pairs={{0,6},{1,7},{2,4},{3,5},{8,14},{9,15},{10,12},{11,13},{16,22},{17,... | collective-permute-start | bytes 786440 | tf_op jit(solution)/shard_map/pivot2/ppermute | solution.py:304
  115.8 16.1 %collective-permute-start.9 = (f32[128,512]{1,0:T(8,128)S(1)}, f32[128,512]{1,0:T(8,128)S(1)}, u32[]{:S(2)}, u32[]{:S(2)}) collective-permute-start(f32[128,512]{1,0:T(8,128)S(1)} %get-tuple-element.71.b0), channel_id=1, source_target_pairs={{0,4},{1,5},{2,6},{3,7},{8,12},{9,13},{10,14},{11,15},{16,20},{17,... | collective-permute-start | bytes 786440 | tf_op jit(solution)/shard_map/pivot2/ppermute | solution.py:304
  117.1 14.9 %collective-permute-start.10 = (f32[128,512]{1,0:T(8,128)S(1)}, f32[128,512]{1,0:T(8,128)S(1)}, u32[]{:S(2)}, u32[]{:S(2)}) collective-permute-start(f32[128,512]{1,0:T(8,128)S(1)} %get-tuple-element.71.b0), channel_id=1, source_target_pairs={{0,1},{1,0},{2,3},{3,2},{4,5},{5,4},{6,7},{7,6},{8,9},{9,8},{10,11... | collective-permute-start | bytes 786440 | tf_op jit(solution)/shard_map/pivot2/ppermute | solution.py:312
  120.4 11.6 %collective-permute-start.11 = (f32[128,512]{1,0:T(8,128)S(1)}, f32[128,512]{1,0:T(8,128)S(1)}, u32[]{:S(2)}, u32[]{:S(2)}) collective-permute-start(f32[128,512]{1,0:T(8,128)S(1)} %collective-permute-done.7.b1), channel_id=1, source_target_pairs={{0,1},{1,0},{2,3},{3,2},{4,5},{5,4},{6,7},{7,6},{8,9},{9,8},{10,11... | collective-permute-start | bytes 786440 | tf_op jit(solution)/shard_map/pivot2/ppermute | solution.py:312
  124.7 8.5 %collective-permute-start.12 = (f32[128,512]{1,0:T(8,128)S(1)}, f32[128,512]{1,0:T(8,128)S(1)}, u32[]{:S(2)}, u32[]{:S(2)}) collective-permute-start(f32[128,512]{1,0:T(8,128)S(1)} %collective-permute-done.8.b2), channel_id=1, source_target_pairs={{0,1},{1,0},{2,3},{3,2},{4,5},{5,4},{6,7},{7,6},{8,9},{9,8},{10,11... | collective-permute-start | bytes 786440 | tf_op jit(solution)/shard_map/pivot2/ppermute | solution.py:312
  132.0 1.5 collective-permute-start.13
  (6 other events, 11.0 us)
Sparse Core Ops, SparseCore 0:
  10.4 35.9 all-gather.2
